TPU v7x, 256 devices: a whole 4x4x8 slice. The times are simulated.
256 devices in a mesh: gx: 16 (over z, y_lo), gy: 16 (over y_hi, x, core).
Axes of the slice: x: 4, y: 4 (y_hi: 2, y_lo: 2; y = y_hi * 2 + y_lo), z: 8, core: 2. Of those that a mesh axis runs over, the one named last changes fastest.
Arguments:
- psi: float32 [64, 128, 4096], P(None, 'gx', 'gy'), may hold values from -500 to 500
- potential: float32 [128, 4096], P('gx', 'gy'), may hold values from -2 to 0
Outputs:
- orbitals: float32 [64, 128, 4096], P(None, 'gx', 'gy')
All inputs are finite; a program needn't handle non-finite values.
Results may differ from a plain program's by a relative error of at most 0.0003.
Values sent between devices are 32-bit elements; how exact they have to be, the bound alone decides.
No kernel may reach another device: no remote copies, remote signals or barrier semaphores. Data moves between devices by JAX's collectives and lax.ppermute only.
A program may use at most 64 MiB of HBM per device.

v0:
```python
import jax
import jax.numpy as jnp
from jax import lax
from jax.sharding import PartitionSpec as P

NZ = 64
COEFS = (-205.0 / 72.0, 8.0 / 5.0, -1.0 / 5.0, 8.0 / 315.0, -1.0 / 560.0)
CENTER = 6.5
HALF_WIDTH = 5.5


def padded(array, sides, width):
    for axis, dim in sides:
        size, length = (lax.axis_size(axis), array.shape[dim])
        up = [(i, (i + 1) % size) for i in range(size)]
        down = [(j, i) for i, j in up]
        last = lax.slice_in_dim(array, length - width, length, axis=dim)
        first = lax.slice_in_dim(array, 0, width, axis=dim)
        before = lax.ppermute(last, axis, up)
        after = lax.ppermute(first, axis, down)
        array = jnp.concatenate([before, array, after], axis=dim)
    return array


def along_third(field, depth_index):
    laplace = 3.0 * COEFS[0] * field
    for distance in range(1, 5):
        forward = jnp.where(
            depth_index < NZ - distance,
            jnp.roll(field, -distance, 2),
            jnp.roll(field, NZ - distance, 2),
        )
        behind = jnp.where(
            depth_index >= distance, jnp.roll(field, distance, 2), jnp.roll(field, distance - NZ, 2)
        )
        laplace = laplace + COEFS[distance] * (forward + behind)
    return laplace


def hamiltonian(field, field_pot, depth_index):
    row_count = field.shape[1]
    lane_count = field.shape[2]
    padded_x = padded(field, (("gx", 1),), 4)
    laplace = along_third(field, depth_index)
    padded_y = padded(field, (("gy", 2),), 4 * NZ)
    for distance in range(1, 5):
        laplace = laplace + COEFS[distance] * (
            padded_x[:, 4 + distance : 4 + distance + row_count]
            + padded_x[:, 4 - distance : 4 - distance + row_count]
        )
        ahead_start = (4 + distance) * NZ
        back_start = (4 - distance) * NZ
        laplace = laplace + COEFS[distance] * (
            padded_y[:, :, ahead_start : ahead_start + lane_count]
            + padded_y[:, :, back_start : back_start + lane_count]
        )
    return -0.5 * laplace + field_pot * field


def orthonormal(matrix, ncount):
    local_gram = jnp.dot(matrix, matrix.T, precision=lax.Precision.HIGHEST) / ncount
    total_gram = lax.psum(local_gram, ("gx", "gy"))
    lower_factor = jnp.linalg.cholesky(total_gram)
    return lax.linalg.triangular_solve(lower_factor, matrix, left_side=True, lower=True)


def on_device(psi, potential):
    orbit_count = psi.shape[0]
    row_count = psi.shape[1]
    lane_count = psi.shape[2]
    field_pot = potential.reshape(1, row_count, lane_count)
    depth_index = lax.broadcasted_iota(jnp.int32, (1, 1, lane_count), 2) % NZ
    level_one = (hamiltonian(psi, field_pot, depth_index) - CENTER * psi) / HALF_WIDTH
    second = (
        2.0 * (hamiltonian(level_one, field_pot, depth_index) - CENTER * level_one) / HALF_WIDTH
        - psi
    )
    filtered = (
        2.0 * (hamiltonian(second, field_pot, depth_index) - CENTER * second) / HALF_WIDTH
        - level_one
    )
    matrix = filtered.reshape(orbit_count, row_count * lane_count)
    ncount = float(row_count * lane_count * lax.axis_size("gx") * lax.axis_size("gy"))
    first_pass = orthonormal(matrix, ncount)
    final_pass = orthonormal(first_pass, ncount)
    return final_pass.reshape(orbit_count, row_count, lane_count)


def solution(mesh):
    in_specs = (P(None, "gx", "gy"), P("gx", "gy"))
    out_specs = P(None, "gx", "gy")
    return jax.shard_map(
        on_device, mesh=mesh, in_specs=in_specs, out_specs=out_specs, check_vma=False
    )
```

profile of v0, /device:TPU:1, one launch (start us, length us, event | category | flops | bytes accessed | tf_op | source)
XLA Modules:
  0.0 262.9 jit_solution(8503108184494606311)
XLA Ops:
  0.0 2.6 collective-permute-start.3
  2.6 0.6 collective-permute-start.2
  3.2 1.3 fusion.198
  4.5 6.0 %collective-permute-start = (f32[64,4,256]{2,1,0:T(4,128)S(1)}, f32[64,4,256]{2,1,0:T(4,128)S(1)}, u32[]{:S(2)}, u32[]{:S(2)}) collective-permute-start(f32[64,4,256]{2,1,0:T(4,128)S(1)} %get-tuple-element.112), channel_id=1, source_target_pairs={{16,0},{32,16},{48,32},{64,48},{80,64},{96,80},{112,96},{128,112},... | collective-permute-start | bytes 786440 | tf_op jit(solution)/shard_map/ppermute | solution.py:20
  10.8 0.2 fusion.194
  11.0 0.2 fusion.197
  11.2 0.2 fusion.182
  11.4 0.2 fusion.185
  11.6 0.2 fusion.186
  11.8 0.2 fusion.189
  13.1 0.6 copy-done.1
  14.2 6.1 %collective-permute-done = f32[64,4,256]{2,1,0:T(4,128)S(1)} collective-permute-done((f32[64,4,256]{2,1,0:T(4,128)S(1)}, f32[64,4,256]{2,1,0:T(4,128)S(1)}, u32[]{:S(2)}, u32[]{:S(2)}) %collective-permute-start) | collective-permute-done | bytes 262176 | tf_op jit(solution)/shard_map/ppermute | solution.py:20
  20.4 3.0 %collective-permute-done.1 = f32[64,4,256]{2,1,0:T(4,128)S(1)} collective-permute-done((f32[64,4,256]{2,1,0:T(4,128)S(1)}, f32[64,4,256]{2,1,0:T(4,128)S(1)}, u32[]{:S(2)}, u32[]{:S(2)}) %collective-permute-start.1) | collective-permute-done | bytes 262176 | tf_op jit(solution)/shard_map/ppermute | solution.py:19
  23.4 3.3 %broadcast_multiply_fusion = (f32[64,8,256]{2,1,0:T(8,128)S(1)}, f32[64,8,256]{2,1,0:T(8,128)S(1)}) fusion(f32[64,8,256]{2,1,0:T(8,128)S(1)} %copy-done, f32[8,256]{1,0:T(8,128)S(1)} %copy-done.1, f32[64,8,256]{2,1,0:T(8,128)S(1)} %collective-permute-done.2, f32[64,8,256]{2,1,0:T(8,128)S(1)} %collective-permute-done.3, ...), kind=kLoop, calls=%fused_computation.221 | loop fusion | flops 9306112 | bytes 16525312 | tf_op jit(solution)/shard_map/div | solution.py:73
  27.0 0.2 fusion.168
  27.2 0.2 fusion.169
  27.4 0.2 fusion.172
  27.6 0.2 fusion.173
  29.2 1.5 collective-permute-start.6
  30.7 0.3 collective-permute-start.7
  31.0 6.1 %collective-permute-start.4 = (f32[64,4,256]{2,1,0:T(4,128)S(1)}, f32[64,4,256]{2,1,0:T(4,128)S(1)}, u32[]{:S(2)}, u32[]{:S(2)}) collective-permute-start(f32[64,4,256]{2,1,0:T(4,128)S(1)} %get-tuple-element.75), channel_id=1, source_target_pairs={{16,0},{32,16},{48,32},{64,48},{80,64},{96,80},{112,96},{128,112},... | collective-permute-start | bytes 786440 | tf_op jit(solution)/shard_map/ppermute | solution.py:20
  37.5 3.5 %collective-permute-done.4 = f32[64,4,256]{2,1,0:T(4,128)S(1)} collective-permute-done((f32[64,4,256]{2,1,0:T(4,128)S(1)}, f32[64,4,256]{2,1,0:T(4,128)S(1)}, u32[]{:S(2)}, u32[]{:S(2)}) %collective-permute-start.4) | collective-permute-done | bytes 262176 | tf_op jit(solution)/shard_map/ppermute | solution.py:20
  41.0 10.6 %collective-permute-done.5 = f32[64,4,256]{2,1,0:T(4,128)S(1)} collective-permute-done((f32[64,4,256]{2,1,0:T(4,128)S(1)}, f32[64,4,256]{2,1,0:T(4,128)S(1)}, u32[]{:S(2)}, u32[]{:S(2)}) %collective-permute-start.5) | collective-permute-done | bytes 262176 | tf_op jit(solution)/shard_map/ppermute | solution.py:19
  51.6 3.7 %fusion.33 = f32[64,8,256]{2,1,0:T(8,128)S(1)} fusion(f32[64,8,256]{2,1,0:T(8,128)S(1)} %copy-done, f32[64,8,256]{2,1,0:T(8,128)S(1)} %collective-permute-done.7, f32[64,8,256]{2,1,0:T(8,128)S(1)} %get-tuple-element.6, f32[64,8,256]{2,1,0:T(8,128)S(1)} %collective-permute-done.6, f32[64,4,256]{2,1,0:T(4,128)S(1)} %collective-permute-done.5, ...), kind=kLoop, calls=%fused_computation.81 | loop fusion | flops 10747904 | bytes 12068864 | tf_op jit(solution)/shard_map/sub | solution.py:75
  55.7 0.2 fusion.152
  56.1 0.2 fusion.156
  56.6 1.3 collective-permute-start.10
  57.9 0.5 collective-permute-start.11
  59.5 4.7 %collective-permute-start.8 = (f32[64,4,256]{2,1,0:T(4,128)S(1)}, f32[64,4,256]{2,1,0:T(4,128)S(1)}, u32[]{:S(2)}, u32[]{:S(2)}) collective-permute-start(f32[64,4,256]{2,1,0:T(4,128)S(1)} %get-tuple-element.41), channel_id=1, source_target_pairs={{16,0},{32,16},{48,32},{64,48},{80,64},{96,80},{112,96},{128,112},... | collective-permute-start | bytes 786440 | tf_op jit(solution)/shard_map/ppermute | solution.py:20
  64.5 0.2 fusion.163
  64.7 3.0 %collective-permute-done.8 = f32[64,4,256]{2,1,0:T(4,128)S(1)} collective-permute-done((f32[64,4,256]{2,1,0:T(4,128)S(1)}, f32[64,4,256]{2,1,0:T(4,128)S(1)}, u32[]{:S(2)}, u32[]{:S(2)}) %collective-permute-start.8) | collective-permute-done | bytes 262176 | tf_op jit(solution)/shard_map/ppermute | solution.py:20
  67.6 12.3 %collective-permute-done.9 = f32[64,4,256]{2,1,0:T(4,128)S(1)} collective-permute-done((f32[64,4,256]{2,1,0:T(4,128)S(1)}, f32[64,4,256]{2,1,0:T(4,128)S(1)}, u32[]{:S(2)}, u32[]{:S(2)}) %collective-permute-start.9) | collective-permute-done | bytes 262176 | tf_op jit(solution)/shard_map/ppermute | solution.py:19
  80.0 3.7 %fusion.13 = f32[64,8,256]{2,1,0:T(8,128)S(1)} fusion(f32[64,8,256]{2,1,0:T(8,128)S(1)} %collective-permute-done.11, f32[64,8,256]{2,1,0:T(8,128)S(1)} %fusion.33, f32[64,8,256]{2,1,0:T(8,128)S(1)} %collective-permute-done.10, f32[64,4,256]{2,1,0:T(4,128)S(1)} %collective-permute-done.9, f32[64,4,256]{2,1,0:T(4,128)S(1)} %collective-permute-done.8, ...), kind=kLoop, calls=%fused_computation.61 | loop fusion | flops 10878976 | bytes 11544576 | tf_op jit(solution)/shard_map/sub | solution.py:79
  83.7 0.7 fusion
  84.4 78.3 %psum.14 = f32[64,64]{0,1:T(8,128)S(1)} all-reduce(f32[64,64]{0,1:T(8,128)S(1)} %fusion), channel_id=1, replica_groups=mesh['gx'=16,'gy'=16] {'gx','gy'}, use_global_device_ids=true, to_apply=%region_0.1 | all-reduce | flops 4096 | bytes 32768 | tf_op jit(solution)/shard_map/psum | solution.py:62
  162.9 5.8 %cholesky.44 = f32[64,64]{1,0:T(8,128)S(1)} custom-call(f32[64,64]{1,0:T(8,128)S(1)} %fusion.144), custom_call_target="Cholesky" | custom-call | tf_op jit(solution)/shard_map/jit(cholesky)/cholesky | solution.py:63
  168.7 0.6 compare_reduce_fusion.1
  169.4 0.7 fusion.137
  170.0 4.9 %custom-call.6 = f32[1,64,64]{1,2,0:T(8,128)S(1)} custom-call(f32[1,64,64]{2,1,0:T(8,128)S(1)} %fusion.137), custom_call_target="InvertDiagBlocksLowerTriangular" | custom-call | tf_op jit(solution)/shard_map/triangular_solve/custom-call.0 | solution.py:64
  175.1 0.6 fusion.142
  175.8 0.6 convolution_multiply_fusion
  176.3 72.7 %psum.15 = f32[64,64]{0,1:T(8,128)S(1)} all-reduce(f32[64,64]{0,1:T(8,128)S(1)} %convolution_multiply_fusion), channel_id=1, replica_groups=mesh['gx'=16,'gy'=16] {'gx','gy'}, use_global_device_ids=true, to_apply=%region_3.6 | all-reduce | flops 4096 | bytes 32768 | tf_op jit(solution)/shard_map/psum | solution.py:62
  249.2 5.8 %cholesky.55 = f32[64,64]{1,0:T(8,128)S(1)} custom-call(f32[64,64]{1,0:T(8,128)S(1)} %fusion.141), custom_call_target="Cholesky" | custom-call | tf_op jit(solution)/shard_map/jit(cholesky)/cholesky | solution.py:63
  255.0 0.6 compare_reduce_fusion
  255.7 0.7 fusion.138
  256.4 4.9 %custom-call.7 = f32[1,64,64]{1,2,0:T(8,128)S(1)} custom-call(f32[1,64,64]{2,1,0:T(8,128)S(1)} %fusion.138), custom_call_target="InvertDiagBlocksLowerTriangular" | custom-call | tf_op jit(solution)/shard_map/triangular_solve/custom-call.0 | solution.py:64
  261.2 0.6 fusion.139
  261.9 1.0 copy.13
  (65 shorter events, 6.3 us)
Async XLA Ops:
  0.0 10.6 %copy-start = (f32[64,8,256]{2,1,0:T(8,128)S(1)}, f32[64,8,256]{2,1,0:T(8,128)}, u32[]{:S(2)}) copy-start(f32[64,8,256]{2,1,0:T(8,128)} %param.5) | copy-start | bytes 1572868
  0.0 13.9 %collective-permute-start.3 = (f32[64,8,256]{2,1,0:T(8,128)}, f32[64,8,256]{2,1,0:T(8,128)S(1)}, u32[]{:S(2)}, u32[]{:S(2)}) collective-permute-start(f32[64,8,256]{2,1,0:T(8,128)} %param.5), channel_id=1, source_target_pairs={{0,1},{1,2},{2,3},{3,4},{4,5},{5,6},{6,7},{7,8},{8,9},{9,10},{10,1... | collective-permute-start | bytes 1572872 | tf_op jit(solution)/shard_map/ppermute | solution.py:19
  2.6 17.7 %collective-permute-start.2 = (f32[64,8,256]{2,1,0:T(8,128)}, f32[64,8,256]{2,1,0:T(8,128)S(1)}, u32[]{:S(2)}, u32[]{:S(2)}) collective-permute-start(f32[64,8,256]{2,1,0:T(8,128)} %param.5), channel_id=1, source_target_pairs={{1,0},{2,1},{3,2},{4,3},{5,4},{6,5},{7,6},{8,7},{9,8},{10,9},{11,1... | collective-permute-start | bytes 1572872 | tf_op jit(solution)/shard_map/ppermute | solution.py:20
  4.5 15.7 %collective-permute-start = (f32[64,4,256]{2,1,0:T(4,128)S(1)}, f32[64,4,256]{2,1,0:T(4,128)S(1)}, u32[]{:S(2)}, u32[]{:S(2)}) collective-permute-start(f32[64,4,256]{2,1,0:T(4,128)S(1)} %get-tuple-element.112), channel_id=1, source_target_pairs={{16,0},{32,16},{48,32},{64,48},{80,64},{96,80},{112,96},{128,112},... | collective-permute-start | bytes 786440 | tf_op jit(solution)/shard_map/ppermute | solution.py:20
  10.6 12.9 %collective-permute-start.1 = (f32[64,4,256]{2,1,0:T(4,128)S(1)}, f32[64,4,256]{2,1,0:T(4,128)S(1)}, u32[]{:S(2)}, u32[]{:S(2)}) collective-permute-start(f32[64,4,256]{2,1,0:T(4,128)S(1)} %get-tuple-element.113), channel_id=1, source_target_pairs={{0,16},{16,32},{32,48},{48,64},{64,80},{80,96},{96,112},{112,128},... | collective-permute-start | bytes 786440 | tf_op jit(solution)/shard_map/ppermute | solution.py:19
  13.0 0.7 copy-start.1
  29.2 22.3 %collective-permute-start.6 = (f32[64,8,256]{2,1,0:T(8,128)S(1)}, f32[64,8,256]{2,1,0:T(8,128)S(1)}, u32[]{:S(2)}, u32[]{:S(2)}) collective-permute-start(f32[64,8,256]{2,1,0:T(8,128)S(1)} %get-tuple-element.6), channel_id=1, source_target_pairs={{1,0},{2,1},{3,2},{4,3},{5,4},{6,5},{7,6},{8,7},{9,8},{10,9},{11,1... | collective-permute-start | bytes 1572872 | tf_op jit(solution)/shard_map/ppermute | solution.py:20
  30.7 20.9 %collective-permute-start.7 = (f32[64,8,256]{2,1,0:T(8,128)S(1)}, f32[64,8,256]{2,1,0:T(8,128)S(1)}, u32[]{:S(2)}, u32[]{:S(2)}) collective-permute-start(f32[64,8,256]{2,1,0:T(8,128)S(1)} %get-tuple-element.6), channel_id=1, source_target_pairs={{0,1},{1,2},{2,3},{3,4},{4,5},{5,6},{6,7},{7,8},{8,9},{9,10},{10,1... | collective-permute-start | bytes 1572872 | tf_op jit(solution)/shard_map/ppermute | solution.py:19
  31.0 10.0 %collective-permute-start.4 = (f32[64,4,256]{2,1,0:T(4,128)S(1)}, f32[64,4,256]{2,1,0:T(4,128)S(1)}, u32[]{:S(2)}, u32[]{:S(2)}) collective-permute-start(f32[64,4,256]{2,1,0:T(4,128)S(1)} %get-tuple-element.75), channel_id=1, source_target_pairs={{16,0},{32,16},{48,32},{64,48},{80,64},{96,80},{112,96},{128,112},... | collective-permute-start | bytes 786440 | tf_op jit(solution)/shard_map/ppermute | solution.py:20
  37.1 14.5 %collective-permute-start.5 = (f32[64,4,256]{2,1,0:T(4,128)S(1)}, f32[64,4,256]{2,1,0:T(4,128)S(1)}, u32[]{:S(2)}, u32[]{:S(2)}) collective-permute-start(f32[64,4,256]{2,1,0:T(4,128)S(1)} %get-tuple-element.76), channel_id=1, source_target_pairs={{0,16},{16,32},{32,48},{48,64},{64,80},{80,96},{96,112},{112,128},... | collective-permute-start | bytes 786440 | tf_op jit(solution)/shard_map/ppermute | solution.py:19
  56.6 23.4 %collective-permute-start.10 = (f32[64,8,256]{2,1,0:T(8,128)S(1)}, f32[64,8,256]{2,1,0:T(8,128)S(1)}, u32[]{:S(2)}, u32[]{:S(2)}) collective-permute-start(f32[64,8,256]{2,1,0:T(8,128)S(1)} %fusion.33), channel_id=1, source_target_pairs={{1,0},{2,1},{3,2},{4,3},{5,4},{6,5},{7,6},{8,7},{9,8},{10,9},{11,1... | collective-permute-start | bytes 1572872 | tf_op jit(solution)/shard_map/ppermute | solution.py:20
  57.9 22.1 %collective-permute-start.11 = (f32[64,8,256]{2,1,0:T(8,128)S(1)}, f32[64,8,256]{2,1,0:T(8,128)S(1)}, u32[]{:S(2)}, u32[]{:S(2)}) collective-permute-start(f32[64,8,256]{2,1,0:T(8,128)S(1)} %fusion.33), channel_id=1, source_target_pairs={{0,1},{1,2},{2,3},{3,4},{4,5},{5,6},{6,7},{7,8},{8,9},{9,10},{10,1... | collective-permute-start | bytes 1572872 | tf_op jit(solution)/shard_map/ppermute | solution.py:19
  59.5 8.1 %collective-permute-start.8 = (f32[64,4,256]{2,1,0:T(4,128)S(1)}, f32[64,4,256]{2,1,0:T(4,128)S(1)}, u32[]{:S(2)}, u32[]{:S(2)}) collective-permute-start(f32[64,4,256]{2,1,0:T(4,128)S(1)} %get-tuple-element.41), channel_id=1, source_target_pairs={{16,0},{32,16},{48,32},{64,48},{80,64},{96,80},{112,96},{128,112},... | collective-permute-start | bytes 786440 | tf_op jit(solution)/shard_map/ppermute | solution.py:20
  64.2 15.7 %collective-permute-start.9 = (f32[64,4,256]{2,1,0:T(4,128)S(1)}, f32[64,4,256]{2,1,0:T(4,128)S(1)}, u32[]{:S(2)}, u32[]{:S(2)}) collective-permute-start(f32[64,4,256]{2,1,0:T(4,128)S(1)} %get-tuple-element.42), channel_id=1, source_target_pairs={{0,16},{16,32},{32,48},{48,64},{64,80},{80,96},{96,112},{112,128},... | collective-permute-start | bytes 786440 | tf_op jit(solution)/shard_map/ppermute | solution.py:19
where the time goes:
time: 263 us
  blocking collectives  151 us (57%)
  waiting for transfers between devices  38.5 us (15%)
  other arithmetic  35 us (13%)
  starting transfers between devices  23.7 us (9%)
  local copies, waits for them, and re-layouts  11.6 us (4%)
    psum x2, blocking collectives, orthonormal(): total_gram = lax.psum(local_gram, ('gx', 'gy'))  151 us
    ppermute x6, waiting for transfers between devices, padded(): before = lax.ppermute(last, axis, up)  25.9 us
    ppermute x6, starting transfers between devices, padded(): after = lax.ppermute(first, axis, down)  20.2 us
    another operation x6, other arithmetic, orthonormal(): lower_factor = jnp.linalg.cholesky(total_gram)  13 us
    ppermute x6, waiting for transfers between devices, padded(): after = lax.ppermute(first, axis, down)  12.5 us
    another operation x4, other arithmetic, orthonormal(): lax.linalg.triangular_solve(lower_factor, matrix, left_side=True, lower=T...  11.1 us
  transfers between devices with their start and end apart: 12, of which 6 were waited for; matrix products, arithmetic and copies ran while one was open for 2% of the time, Pallas kernels for 0%

commit v1 on v0

--- a/solution.py
+++ b/solution.py
@@ -59,7 +59,8 @@
 
 def orthonormal(matrix, ncount):
     local_gram = jnp.dot(matrix, matrix.T, precision=lax.Precision.HIGHEST) / ncount
-    total_gram = lax.psum(local_gram, ("gx", "gy"))
+    inner = lax.psum(local_gram, "gy")
+    total_gram = lax.psum(inner, "gx")
     lower_factor = jnp.linalg.cholesky(total_gram)
     return lax.linalg.triangular_solve(lower_factor, matrix, left_side=True, lower=True)
 

time: 263 us -> 369 us (1.40)
  the two profiles are of different devices: /device:TPU:1 before, /device:TPU:16 now
where the time goes in v1:
time: 369 us; the launch traced here: 368 us
  blocking collectives  258 us (70%)
  other arithmetic  35.3 us (10%)
  starting transfers between devices  32.2 us (9%)
  waiting for transfers between devices  27.8 us (8%)
  local copies, waits for them, and re-layouts  11.6 us (3%)
    psum x2, blocking collectives, orthonormal(): inner = lax.psum(local_gram, 'gy')  132 us
    psum x2, blocking collectives, orthonormal(): total_gram = lax.psum(inner, 'gx')  126 us
    ppermute x6, starting transfers between devices, padded(): after = lax.ppermute(first, axis, down)  32.2 us
    ppermute x6, waiting for transfers between devices, padded(): after = lax.ppermute(first, axis, down)  27.8 us
    another operation x6, other arithmetic, orthonormal(): lower_factor = jnp.linalg.cholesky(total_gram)  13 us
    another operation x4, other arithmetic, orthonormal(): lax.linalg.triangular_solve(lower_factor, matrix, left_side=True, lower=T...  11.1 us
  transfers between devices with their start and end apart: 12, of which 3 were waited for; matrix products, arithmetic and copies ran while one was open for 2% of the time, Pallas kernels for 0%

profile of v1, /device:TPU:16, one launch (start us, length us, event | category | flops | bytes accessed | tf_op | source)
XLA Modules:
  0.0 368.4 jit_solution(14094657103007111270)
XLA Ops:
  0.0 5.4 %collective-permute-start.2 = (f32[64,8,256]{2,1,0:T(8,128)}, f32[64,8,256]{2,1,0:T(8,128)S(1)}, u32[]{:S(2)}, u32[]{:S(2)}) collective-permute-start(f32[64,8,256]{2,1,0:T(8,128)} %param.5), channel_id=1, source_target_pairs={{1,0},{2,1},{3,2},{4,3},{5,4},{6,5},{7,6},{8,7},{9,8},{10,9},{11,1... | collective-permute-start | bytes 1572872 | tf_op jit(solution)/shard_map/ppermute | solution.py:20
  5.4 1.3 fusion.198
  6.7 6.7 %collective-permute-start = (f32[64,4,256]{2,1,0:T(4,128)S(1)}, f32[64,4,256]{2,1,0:T(4,128)S(1)}, u32[]{:S(2)}, u32[]{:S(2)}) collective-permute-start(f32[64,4,256]{2,1,0:T(4,128)S(1)} %get-tuple-element.112), channel_id=1, source_target_pairs={{16,0},{32,16},{48,32},{64,48},{80,64},{96,80},{112,96},{128,112},... | collective-permute-start | bytes 786440 | tf_op jit(solution)/shard_map/ppermute | solution.py:20
  13.5 0.2 fusion.194
  13.7 0.2 fusion.197
  13.9 0.2 fusion.182
  14.1 0.2 fusion.185
  14.3 0.2 fusion.186
  14.6 0.2 fusion.189
  15.9 0.6 copy-done.1
  16.9 5.5 %collective-permute-done = f32[64,4,256]{2,1,0:T(4,128)S(1)} collective-permute-done((f32[64,4,256]{2,1,0:T(4,128)S(1)}, f32[64,4,256]{2,1,0:T(4,128)S(1)}, u32[]{:S(2)}, u32[]{:S(2)}) %collective-permute-start) | collective-permute-done | bytes 262176 | tf_op jit(solution)/shard_map/ppermute | solution.py:20
  22.6 3.4 broadcast_multiply_fusion
  26.2 0.2 fusion.168
  26.5 0.2 fusion.169
  26.7 0.2 fusion.172
  26.9 0.2 fusion.173
  27.1 0.2 fusion.176
  28.5 3.1 collective-permute-start.6
  31.6 7.7 %collective-permute-start.4 = (f32[64,4,256]{2,1,0:T(4,128)S(1)}, f32[64,4,256]{2,1,0:T(4,128)S(1)}, u32[]{:S(2)}, u32[]{:S(2)}) collective-permute-start(f32[64,4,256]{2,1,0:T(4,128)S(1)} %get-tuple-element.75), channel_id=1, source_target_pairs={{16,0},{32,16},{48,32},{64,48},{80,64},{96,80},{112,96},{128,112},... | collective-permute-start | bytes 786440 | tf_op jit(solution)/shard_map/ppermute | solution.py:20
  39.5 0.2 fusion.180
  39.7 10.2 %collective-permute-done.4 = f32[64,4,256]{2,1,0:T(4,128)S(1)} collective-permute-done((f32[64,4,256]{2,1,0:T(4,128)S(1)}, f32[64,4,256]{2,1,0:T(4,128)S(1)}, u32[]{:S(2)}, u32[]{:S(2)}) %collective-permute-start.4) | collective-permute-done | bytes 262176 | tf_op jit(solution)/shard_map/ppermute | solution.py:20
  49.9 3.8 %fusion.33 = f32[64,8,256]{2,1,0:T(8,128)S(1)} fusion(f32[64,8,256]{2,1,0:T(8,128)S(1)} %copy-done, f32[64,8,256]{2,1,0:T(8,128)S(1)} %collective-permute-done.7, f32[64,8,256]{2,1,0:T(8,128)S(1)} %get-tuple-element.6, f32[64,8,256]{2,1,0:T(8,128)S(1)} %collective-permute-done.6, f32[64,4,256]{2,1,0:T(4,128)S(1)} %collective-permute-done.5, ...), kind=kLoop, calls=%fused_computation.81 | loop fusion | flops 10747904 | bytes 12068864 | tf_op jit(solution)/shard_map/sub | solution.py:76
  54.0 0.2 fusion.151
  54.2 0.2 fusion.152
  54.4 0.2 fusion.155
  54.6 0.2 fusion.156
  54.8 0.2 fusion.159
  55.1 3.2 collective-permute-start.10
  59.4 6.1 %collective-permute-start.8 = (f32[64,4,256]{2,1,0:T(4,128)S(1)}, f32[64,4,256]{2,1,0:T(4,128)S(1)}, u32[]{:S(2)}, u32[]{:S(2)}) collective-permute-start(f32[64,4,256]{2,1,0:T(4,128)S(1)} %get-tuple-element.41), channel_id=1, source_target_pairs={{16,0},{32,16},{48,32},{64,48},{80,64},{96,80},{112,96},{128,112},... | collective-permute-start | bytes 786440 | tf_op jit(solution)/shard_map/ppermute | solution.py:20
  66.0 12.0 %collective-permute-done.8 = f32[64,4,256]{2,1,0:T(4,128)S(1)} collective-permute-done((f32[64,4,256]{2,1,0:T(4,128)S(1)}, f32[64,4,256]{2,1,0:T(4,128)S(1)}, u32[]{:S(2)}, u32[]{:S(2)}) %collective-permute-start.8) | collective-permute-done | bytes 262176 | tf_op jit(solution)/shard_map/ppermute | solution.py:20
  78.0 3.8 %fusion.13 = f32[64,8,256]{2,1,0:T(8,128)S(1)} fusion(f32[64,8,256]{2,1,0:T(8,128)S(1)} %collective-permute-done.11, f32[64,8,256]{2,1,0:T(8,128)S(1)} %fusion.33, f32[64,8,256]{2,1,0:T(8,128)S(1)} %collective-permute-done.10, f32[64,4,256]{2,1,0:T(4,128)S(1)} %collective-permute-done.9, f32[64,4,256]{2,1,0:T(4,128)S(1)} %collective-permute-done.8, ...), kind=kLoop, calls=%fused_computation.61 | loop fusion | flops 10878976 | bytes 11544576 | tf_op jit(solution)/shard_map/sub | solution.py:80
  81.9 0.7 fusion
  82.6 67.3 %psum.28 = f32[64,64]{0,1:T(8,128)S(1)} all-reduce(f32[64,64]{0,1:T(8,128)S(1)} %fusion), channel_id=1, replica_groups=mesh['gx'=16,'gy'=16] {'gy'}, use_global_device_ids=true, to_apply=%region_0.1 | all-reduce | flops 4096 | bytes 32768 | tf_op jit(solution)/shard_map/psum | solution.py:62
  149.9 66.3 %psum.29 = f32[64,64]{0,1:T(8,128)S(1)} all-reduce(f32[64,64]{0,1:T(8,128)S(1)} %psum.28), channel_id=1, replica_groups=mesh['gx'=16,'gy'=16] {'gx'}, use_global_device_ids=true, to_apply=%region_1.2 | all-reduce | flops 4096 | bytes 32768 | tf_op jit(solution)/shard_map/psum | solution.py:63
  216.3 5.8 %cholesky.44 = f32[64,64]{1,0:T(8,128)S(1)} custom-call(f32[64,64]{1,0:T(8,128)S(1)} %fusion.144), custom_call_target="Cholesky" | custom-call | tf_op jit(solution)/shard_map/jit(cholesky)/cholesky | solution.py:64
  222.2 0.6 compare_reduce_fusion.1
  222.8 0.7 fusion.137
  223.5 4.9 %custom-call.6 = f32[1,64,64]{1,2,0:T(8,128)S(1)} custom-call(f32[1,64,64]{2,1,0:T(8,128)S(1)} %fusion.137), custom_call_target="InvertDiagBlocksLowerTriangular" | custom-call | tf_op jit(solution)/shard_map/triangular_solve/custom-call.0 | solution.py:65
  228.6 0.6 fusion.142
  229.2 0.6 convolution_multiply_fusion
  229.8 65.0 %psum.30 = f32[64,64]{0,1:T(8,128)S(1)} all-reduce(f32[64,64]{0,1:T(8,128)S(1)} %convolution_multiply_fusion), channel_id=1, replica_groups=mesh['gx'=16,'gy'=16] {'gy'}, use_global_device_ids=true, to_apply=%region_4.7 | all-reduce | flops 4096 | bytes 32768 | tf_op jit(solution)/shard_map/psum | solution.py:62
  294.7 59.8 %psum.31 = f32[64,64]{0,1:T(8,128)S(1)} all-reduce(f32[64,64]{0,1:T(8,128)S(1)} %psum.30), channel_id=1, replica_groups=mesh['gx'=16,'gy'=16] {'gx'}, use_global_device_ids=true, to_apply=%region_5.8 | all-reduce | flops 4096 | bytes 32768 | tf_op jit(solution)/shard_map/psum | solution.py:63
  354.7 5.8 %cholesky.55 = f32[64,64]{1,0:T(8,128)S(1)} custom-call(f32[64,64]{1,0:T(8,128)S(1)} %fusion.141), custom_call_target="Cholesky" | custom-call | tf_op jit(solution)/shard_map/jit(cholesky)/cholesky | solution.py:64
  360.6 0.6 compare_reduce_fusion
  361.2 0.7 fusion.138
  361.9 4.9 %custom-call.7 = f32[1,64,64]{1,2,0:T(8,128)S(1)} custom-call(f32[1,64,64]{2,1,0:T(8,128)S(1)} %fusion.138), custom_call_target="InvertDiagBlocksLowerTriangular" | custom-call | tf_op jit(solution)/shard_map/triangular_solve/custom-call.0 | solution.py:65
  366.8 0.6 fusion.139
  367.4 1.0 copy.13
  (67 shorter events, 5.5 us)
Async XLA Ops:
  0.0 13.3 %copy-start = (f32[64,8,256]{2,1,0:T(8,128)S(1)}, f32[64,8,256]{2,1,0:T(8,128)}, u32[]{:S(2)}) copy-start(f32[64,8,256]{2,1,0:T(8,128)} %param.5) | copy-start | bytes 1572868
  0.0 16.7 %collective-permute-start.3 = (f32[64,8,256]{2,1,0:T(8,128)}, f32[64,8,256]{2,1,0:T(8,128)S(1)}, u32[]{:S(2)}, u32[]{:S(2)}) collective-permute-start(f32[64,8,256]{2,1,0:T(8,128)} %param.5), channel_id=1, source_target_pairs={{0,1},{1,2},{2,3},{3,4},{4,5},{5,6},{6,7},{7,8},{8,9},{9,10},{10,1... | collective-permute-start | bytes 1572872 | tf_op jit(solution)/shard_map/ppermute | solution.py:19
  0.0 22.5 %collective-permute-start.2 = (f32[64,8,256]{2,1,0:T(8,128)}, f32[64,8,256]{2,1,0:T(8,128)S(1)}, u32[]{:S(2)}, u32[]{:S(2)}) collective-permute-start(f32[64,8,256]{2,1,0:T(8,128)} %param.5), channel_id=1, source_target_pairs={{1,0},{2,1},{3,2},{4,3},{5,4},{6,5},{7,6},{8,7},{9,8},{10,9},{11,1... | collective-permute-start | bytes 1572872 | tf_op jit(solution)/shard_map/ppermute | solution.py:20
  6.7 15.8 %collective-permute-start = (f32[64,4,256]{2,1,0:T(4,128)S(1)}, f32[64,4,256]{2,1,0:T(4,128)S(1)}, u32[]{:S(2)}, u32[]{:S(2)}) collective-permute-start(f32[64,4,256]{2,1,0:T(4,128)S(1)} %get-tuple-element.112), channel_id=1, source_target_pairs={{16,0},{32,16},{48,32},{64,48},{80,64},{96,80},{112,96},{128,112},... | collective-permute-start | bytes 786440 | tf_op jit(solution)/shard_map/ppermute | solution.py:20
  13.3 9.3 %collective-permute-start.1 = (f32[64,4,256]{2,1,0:T(4,128)S(1)}, f32[64,4,256]{2,1,0:T(4,128)S(1)}, u32[]{:S(2)}, u32[]{:S(2)}) collective-permute-start(f32[64,4,256]{2,1,0:T(4,128)S(1)} %get-tuple-element.113), channel_id=1, source_target_pairs={{0,16},{16,32},{32,48},{48,64},{64,80},{80,96},{96,112},{112,128},... | collective-permute-start | bytes 786440 | tf_op jit(solution)/shard_map/ppermute | solution.py:19
  15.7 0.7 copy-start.1
  28.5 21.5 %collective-permute-start.6 = (f32[64,8,256]{2,1,0:T(8,128)S(1)}, f32[64,8,256]{2,1,0:T(8,128)S(1)}, u32[]{:S(2)}, u32[]{:S(2)}) collective-permute-start(f32[64,8,256]{2,1,0:T(8,128)S(1)} %get-tuple-element.6), channel_id=1, source_target_pairs={{1,0},{2,1},{3,2},{4,3},{5,4},{6,5},{7,6},{8,7},{9,8},{10,9},{11,1... | collective-permute-start | bytes 1572872 | tf_op jit(solution)/shard_map/ppermute | solution.py:20
  31.6 18.3 %collective-permute-start.7 = (f32[64,8,256]{2,1,0:T(8,128)S(1)}, f32[64,8,256]{2,1,0:T(8,128)S(1)}, u32[]{:S(2)}, u32[]{:S(2)}) collective-permute-start(f32[64,8,256]{2,1,0:T(8,128)S(1)} %get-tuple-element.6), channel_id=1, source_target_pairs={{0,1},{1,2},{2,3},{3,4},{4,5},{5,6},{6,7},{7,8},{8,9},{9,10},{10,1... | collective-permute-start | bytes 1572872 | tf_op jit(solution)/shard_map/ppermute | solution.py:19
  31.6 18.3 %collective-permute-start.4 = (f32[64,4,256]{2,1,0:T(4,128)S(1)}, f32[64,4,256]{2,1,0:T(4,128)S(1)}, u32[]{:S(2)}, u32[]{:S(2)}) collective-permute-start(f32[64,4,256]{2,1,0:T(4,128)S(1)} %get-tuple-element.75), channel_id=1, source_target_pairs={{16,0},{32,16},{48,32},{64,48},{80,64},{96,80},{112,96},{128,112},... | collective-permute-start | bytes 786440 | tf_op jit(solution)/shard_map/ppermute | solution.py:20
  39.3 10.6 %collective-permute-start.5 = (f32[64,4,256]{2,1,0:T(4,128)S(1)}, f32[64,4,256]{2,1,0:T(4,128)S(1)}, u32[]{:S(2)}, u32[]{:S(2)}) collective-permute-start(f32[64,4,256]{2,1,0:T(4,128)S(1)} %get-tuple-element.76), channel_id=1, source_target_pairs={{0,16},{16,32},{32,48},{48,64},{64,80},{80,96},{96,112},{112,128},... | collective-permute-start | bytes 786440 | tf_op jit(solution)/shard_map/ppermute | solution.py:19
  55.1 22.9 %collective-permute-start.10 = (f32[64,8,256]{2,1,0:T(8,128)S(1)}, f32[64,8,256]{2,1,0:T(8,128)S(1)}, u32[]{:S(2)}, u32[]{:S(2)}) collective-permute-start(f32[64,8,256]{2,1,0:T(8,128)S(1)} %fusion.33), channel_id=1, source_target_pairs={{1,0},{2,1},{3,2},{4,3},{5,4},{6,5},{7,6},{8,7},{9,8},{10,9},{11,1... | collective-permute-start | bytes 1572872 | tf_op jit(solution)/shard_map/ppermute | solution.py:20
  58.3 19.7 %collective-permute-start.11 = (f32[64,8,256]{2,1,0:T(8,128)S(1)}, f32[64,8,256]{2,1,0:T(8,128)S(1)}, u32[]{:S(2)}, u32[]{:S(2)}) collective-permute-start(f32[64,8,256]{2,1,0:T(8,128)S(1)} %fusion.33), channel_id=1, source_target_pairs={{0,1},{1,2},{2,3},{3,4},{4,5},{5,6},{6,7},{7,8},{8,9},{9,10},{10,1... | collective-permute-start | bytes 1572872 | tf_op jit(solution)/shard_map/ppermute | solution.py:19
  59.4 18.6 %collective-permute-start.8 = (f32[64,4,256]{2,1,0:T(4,128)S(1)}, f32[64,4,256]{2,1,0:T(4,128)S(1)}, u32[]{:S(2)}, u32[]{:S(2)}) collective-permute-start(f32[64,4,256]{2,1,0:T(4,128)S(1)} %get-tuple-element.41), channel_id=1, source_target_pairs={{16,0},{32,16},{48,32},{64,48},{80,64},{96,80},{112,96},{128,112},... | collective-permute-start | bytes 786440 | tf_op jit(solution)/shard_map/ppermute | solution.py:20
  65.6 12.5 %collective-permute-start.9 = (f32[64,4,256]{2,1,0:T(4,128)S(1)}, f32[64,4,256]{2,1,0:T(4,128)S(1)}, u32[]{:S(2)}, u32[]{:S(2)}) collective-permute-start(f32[64,4,256]{2,1,0:T(4,128)S(1)} %get-tuple-element.42), channel_id=1, source_target_pairs={{0,16},{16,32},{32,48},{48,64},{64,80},{80,96},{96,112},{112,128},... | collective-permute-start | bytes 786440 | tf_op jit(solution)/shard_map/ppermute | solution.py:19
